TPU v7x, 32 devices: a whole 2x2x4 slice. The times are simulated.
32 devices in a mesh: groups: 2 (over x), seq: 16 (over z, y, core).
Axes of the slice: x: 2, y: 2, z: 4, core: 2. Of those that a mesh axis runs over, the one named last changes fastest.
Arguments:
- sequence: bfloat16 [8192, 1536], P(('groups', 'seq')), parts along dimension 0, may hold values from -6 to 6
- gain_conv: float32 [1536], replicated, may hold values from 0.25 to 1.75
- conv_weight: float32 [5, 1536], replicated, may hold values from -3 to 3
- gain_attn: float32 [1536], replicated, may hold values from 0.25 to 1.75
- w_query: bfloat16 [1536, 1024], replicated
- w_key: bfloat16 [1536, 128], replicated
- w_value: bfloat16 [1536, 192], replicated, may hold values from -0.15625 to 0.15625
- w_out: bfloat16 [1536, 1536], replicated, may hold values from -0.15625 to 0.15625
- w_left: bfloat16 [1536, 128], replicated, may hold values from -0.15625 to 0.15625
- w_right: bfloat16 [1536, 128], replicated, may hold values from -0.15625 to 0.15625
- w_pair: bfloat16 [3, 3, 128, 128], replicated, may hold values from -0.1875 to 0.1875
Outputs:
- track: bfloat16 [8192, 1536], P(('groups', 'seq')), parts along dimension 0
- pair_map: bfloat16 [512, 256, 128], P(('groups', 'seq')), parts along dimension 0
There are 2 independent parts, one for each index of `groups`. A program takes and returns all parts, laid end to end along the dimension named above; an argument that names none is the same for every part. Nothing has to cross between parts.
All inputs are finite; a program needn't handle non-finite values.
Results may differ from a plain program's by a relative error of at most 0.019.
Values may be sent and summed in bfloat16 or wider, within the bound.
A program may use at most 128 MiB of HBM per device.

v0:
```python
import jax
import jax.numpy as jnp
from jax import lax
from jax.sharding import PartitionSpec as P

HEADS = 8
POOL = 16


def extended_2(cells, sides, width):
    for axis, dim in sides:
        count = lax.axis_size(axis)
        ends = count - 1
        head = lax.slice_in_dim(cells, 0, width, axis=dim)
        tail = lax.slice_in_dim(cells, cells.shape[dim] - width, cells.shape[dim], axis=dim)
        cells = jnp.concatenate(
            [
                lax.ppermute(tail, axis, [(i, (i + 1) % count) for i in range(ends)]),
                cells,
                lax.ppermute(head, axis, [((i + 1) % count, i) for i in range(ends)]),
            ],
            axis=dim,
        )
    return cells


def rms_norm(values, gain):
    values = values.astype(jnp.float32)
    scale = lax.rsqrt(jnp.mean(values * values, axis=-1, keepdims=True) + 1e-06)
    return values * scale * gain


def attend_block(carry, queries, keys_part, values_part):
    running, totals, numer = carry
    scale = 1.0 / jnp.sqrt(jnp.float32(queries.shape[2]))
    scores = (
        jnp.einsum("qhd,kd->hqk", queries, keys_part, preferred_element_type=jnp.float32) * scale
    )
    newtop = jnp.maximum(running, jnp.max(scores, axis=-1))
    expo = jnp.exp(scores - newtop[..., None])
    factor = jnp.exp(running - newtop)
    totals = totals * factor + jnp.sum(expo, axis=-1)
    numer = numer * factor[..., None] + jnp.einsum(
        "hqk,kv->hqv", expo.astype(jnp.bfloat16), values_part, preferred_element_type=jnp.float32
    )
    return (newtop, totals, numer)


def attend_piece(carry, queries, keys_part, values_part):
    length = keys_part.shape[0]
    key_blocks = keys_part.reshape(length // 512, 512, keys_part.shape[1])
    value_blocks = values_part.reshape(length // 512, 512, values_part.shape[1])

    def stepper(state, blocks):
        return (attend_block(state, queries, blocks[0], blocks[1]), None)

    carry, unused = lax.scan(stepper, carry, (key_blocks, value_blocks))
    return carry


def local(
    sequence,
    gain_conv,
    conv_weight,
    gain_attn,
    w_query,
    w_key,
    w_value,
    w_out,
    w_left,
    w_right,
    w_pair,
):
    rows = sequence.shape[0]
    width = sequence.shape[1]
    heads = HEADS
    key_size = w_key.shape[1]
    value_size = w_value.shape[1]
    normed = rms_norm(sequence, gain_conv).astype(jnp.bfloat16)
    padded = extended_2(normed, (("seq", 0),), 2)
    convolved = jnp.zeros((rows, width), jnp.float32)
    for offset in range(conv_weight.shape[0]):
        convolved = convolved + conv_weight[offset][None, :] * padded[
            offset : offset + rows
        ].astype(jnp.float32)
    first = (sequence.astype(jnp.float32) + convolved).astype(jnp.bfloat16)
    attn_in = rms_norm(first, gain_attn).astype(jnp.bfloat16)
    queries = (
        jnp.dot(attn_in, w_query, preferred_element_type=jnp.float32)
        .astype(jnp.bfloat16)
        .reshape(rows, heads, key_size)
    )
    initial = (
        jnp.full((heads, rows), -1e30, jnp.float32),
        jnp.zeros((heads, rows), jnp.float32),
        jnp.zeros((heads, rows, value_size), jnp.float32),
    )
    keys_local = jnp.dot(attn_in, w_key, preferred_element_type=jnp.float32).astype(jnp.bfloat16)
    values_local = jnp.dot(attn_in, w_value, preferred_element_type=jnp.float32).astype(
        jnp.bfloat16
    )
    running, totals, numer = attend_piece(
        initial,
        queries,
        lax.all_gather(keys_local, "seq", axis=0, tiled=True),
        lax.all_gather(values_local, "seq", axis=0, tiled=True),
    )
    result = numer / totals[..., None]
    attended = (
        jnp.transpose(result, (1, 0, 2)).reshape(rows, heads * value_size).astype(jnp.bfloat16)
    )
    track = (
        first.astype(jnp.float32) + jnp.dot(attended, w_out, preferred_element_type=jnp.float32)
    ).astype(jnp.bfloat16)
    pooled = jnp.mean(track.astype(jnp.float32).reshape(rows // POOL, POOL, width), axis=1).astype(
        jnp.bfloat16
    )
    left = jnp.dot(pooled, w_left, preferred_element_type=jnp.float32).astype(jnp.bfloat16)
    right = jnp.dot(pooled, w_right, preferred_element_type=jnp.float32).astype(jnp.bfloat16)
    band = left.shape[0]
    right_all = lax.all_gather(right, "seq", axis=0, tiled=True)
    pair0 = (
        left.astype(jnp.float32)[:, None, :] * right_all.astype(jnp.float32)[None, :, :]
    ).astype(jnp.bfloat16)
    activated = jax.nn.gelu(pair0.astype(jnp.float32)).astype(jnp.bfloat16)
    extended = extended_2(activated, (("seq", 0),), 1)
    columns = right_all.shape[0]
    channels = right_all.shape[1]
    grid = jnp.pad(extended, ((0, 0), (1, 1), (0, 0)))
    summed = jnp.zeros((band * columns, channels), jnp.float32)
    for row_off in range(3):
        for col_off in range(3):
            window = grid[row_off : row_off + band, col_off : col_off + columns].reshape(
                band * columns, channels
            )
            summed = summed + jnp.dot(
                window, w_pair[row_off, col_off], preferred_element_type=jnp.float32
            )
    pair_map = (pair0.astype(jnp.float32) + summed.reshape(band, columns, channels)).astype(
        jnp.bfloat16
    )
    return (track, pair_map)


def solution(mesh):
    placed = (P(("groups", "seq"), None), P(), P(), P(), P(), P(), P(), P(), P(), P(), P())
    return jax.shard_map(
        local,
        mesh=mesh,
        in_specs=placed,
        out_specs=(P(("groups", "seq"), None), P(("groups", "seq"), None, None)),
        check_vma=False,
    )
```

profile of v0, /device:TPU:0, one launch (start us, length us, event | category | flops | bytes accessed | tf_op | source)
XLA Modules:
  0.0 202.6 jit_solution(1153907717193346455)
XLA Ops:
  7.2 1.5 fusion.29
  10.3 2.4 %collective-permute-start = (bf16[2,1536]{1,0:T(2,128)(2,1)S(1)}, bf16[2,1536]{1,0:T(2,128)(2,1)S(1)}, u32[]{:S(2)}, u32[]{:S(2)}) collective-permute-start(bf16[2,1536]{1,0:T(2,128)(2,1)S(1)} %get-tuple-element.108), channel_id=1, source_target_pairs={{0,1},{1,2},{2,3},{3,4},{4,5},{5,6},{6,7},{7,8},{8,9},{9,10},{10,1... | collective-permute-start | bytes 18440 | tf_op jit(solution)/shard_map/ppermute | solution.py:18
  14.1 3.8 %collective-permute-done.1 = bf16[2,1536]{1,0:T(2,128)(2,1)S(1)} collective-permute-done((bf16[2,1536]{1,0:T(2,128)(2,1)S(1)}, bf16[2,1536]{1,0:T(2,128)(2,1)S(1)}, u32[]{:S(2)}, u32[]{:S(2)}) %collective-permute-start.1) | collective-permute-done | bytes 6176 | tf_op jit(solution)/shard_map/ppermute | solution.py:20
  17.9 1.6 fusion.33
  21.5 2.3 %convolution_convert_fusion.2 = bf16[256,128]{1,0:T(8,128)(2,1)} fusion(bf16[1536,128]{1,0:T(8,128)(2,1)} %param.18, bf16[256,1536]{1,0:T(8,128)(2,1)} %copy-done.4, f32[1536]{0:T(1024)S(1)} %copy-done.11, f32[256]{0:T(256)S(1)} %add_rsqrt_fusion), kind=kOutput, calls=%fused_computation.71 | convolution fusion | flops 102268928 | bytes 1252352 | tf_op jit(solution)/shard_map/dot_general | solution.py:98
  23.9 2.2 %fusion.39 = bf16[32,8,8,128]{3,2,1,0:T(8,128)(2,1)S(1)} fusion(bf16[1536,1024]{1,0:T(8,128)(2,1)S(1)} %copy-done, bf16[256,1536]{1,0:T(8,128)(2,1)} %copy-done.4, f32[1536]{0:T(1024)S(1)} %copy-done.11, f32[256]{0:T(256)S(1)} %add_rsqrt_fusion), kind=kOutput, calls=%fused_computation.67 | convolution fusion | flops 807141376 | bytes 4463616 | tf_op jit(solution)/shard_map/dot_general | solution.py:89
  26.9 36.6 %all-gather.5.cloned.1.call-done = bf16[4096,192]{0,1:T(8,128)(2,1)} async-done(((bf16[256,192]{0,1:T(8,128)(2,1)}), bf16[4096,192]{0,1:T(8,128)(2,1)}) %all-gather.5.cloned.1.call-update) | async-done | bytes 1572880 | tf_op jit(solution)/shard_map/all_gather | solution.py:106
  63.5 2.7 %copy.21 = bf16[24,8,8,512]{3,2,0,1:T(8,128)(2,1)} copy(bf16[24,8,8,512]{3,2,1,0:T(8,128)(2,1)} %bitcast.116) | data formatting | bytes 3145728 | tf_op jit(solution)/shard_map/reshape | solution.py:52
  66.3 36.7 %all-gather.3.cloned.1.call-done = bf16[4096,128]{1,0:T(8,128)(2,1)} async-done(((bf16[256,128]{1,0:T(8,128)(2,1)}), bf16[4096,128]{1,0:T(8,128)(2,1)}) %all-gather.3.cloned.1.call-update) | async-done | bytes 1048592 | tf_op jit(solution)/shard_map/all_gather | solution.py:105
  103.0 53.1 %while.15 = (s32[]{:T(128)}, f32[8,256]{1,0:T(8,128)S(1)}, f32[8,256]{1,0:T(8,128)S(1)}, f32[8,256,192]{1,2,0:T(8,128)}, bf16[8,512,128]{2,1,0:T(8,128)(2,1)}, /...) while((s32[]{:T(128)}, f32[8,256]{1,0:T(8,128)S(1)}, ...), condition=%wide.region_5.6_spmd.clone, body=%wide.region_2.5_spmd.clone.sunk | while | flops 680667136 | bytes 29294768 | solution.py:57
  103.0 1.8 bitcast_reduce_fusion.2
  106.3 2.2 %fusion.102 = f32[8,256,192]{1,2,0:T(8,128)S(1)} fusion(f32[8,256,192]{1,2,0:T(8,128)S(1)} %copy-done.1, f32[512,256,8]{1,0,2:T(8,128)S(1)} %get-tuple-element.160, f32[8,256]{1,0:T(8,128)S(1)} %select_maximum_fusion.2, f32[8,256]{1,0:T(8,128)S(1)} %get-tuple-element.162, pred[]{:T(512)S(6)} %compare.44, ...), kind=kOutput, calls=%fused_computation.9.clone.1 | convolution fusion | flops 406978560 | bytes 7553029 | tf_op jit(solution)/shard_map/while/body/eval_jaxpr/hqk,kv->hqv/dot_general | solution.py:43
  109.6 1.8 bitcast_reduce_fusion.2
  112.9 2.2 %fusion.102 = f32[8,256,192]{1,2,0:T(8,128)S(1)} fusion(f32[8,256,192]{1,2,0:T(8,128)S(1)} %copy-done.1, f32[512,256,8]{1,0,2:T(8,128)S(1)} %get-tuple-element.160, f32[8,256]{1,0:T(8,128)S(1)} %select_maximum_fusion.2, f32[8,256]{1,0:T(8,128)S(1)} %get-tuple-element.162, pred[]{:T(512)S(6)} %compare.44, ...), kind=kOutput, calls=%fused_computation.9.clone.1 | convolution fusion | flops 406978560 | bytes 7553029 | tf_op jit(solution)/shard_map/while/body/eval_jaxpr/hqk,kv->hqv/dot_general | solution.py:43
  116.3 1.8 bitcast_reduce_fusion.2
  119.5 2.2 %fusion.102 = f32[8,256,192]{1,2,0:T(8,128)S(1)} fusion(f32[8,256,192]{1,2,0:T(8,128)S(1)} %copy-done.1, f32[512,256,8]{1,0,2:T(8,128)S(1)} %get-tuple-element.160, f32[8,256]{1,0:T(8,128)S(1)} %select_maximum_fusion.2, f32[8,256]{1,0:T(8,128)S(1)} %get-tuple-element.162, pred[]{:T(512)S(6)} %compare.44, ...), kind=kOutput, calls=%fused_computation.9.clone.1 | convolution fusion | flops 406978560 | bytes 7553029 | tf_op jit(solution)/shard_map/while/body/eval_jaxpr/hqk,kv->hqv/dot_general | solution.py:43
  122.9 1.8 bitcast_reduce_fusion.2
  126.2 2.2 %fusion.102 = f32[8,256,192]{1,2,0:T(8,128)S(1)} fusion(f32[8,256,192]{1,2,0:T(8,128)S(1)} %copy-done.1, f32[512,256,8]{1,0,2:T(8,128)S(1)} %get-tuple-element.160, f32[8,256]{1,0:T(8,128)S(1)} %select_maximum_fusion.2, f32[8,256]{1,0:T(8,128)S(1)} %get-tuple-element.162, pred[]{:T(512)S(6)} %compare.44, ...), kind=kOutput, calls=%fused_computation.9.clone.1 | convolution fusion | flops 406978560 | bytes 7553029 | tf_op jit(solution)/shard_map/while/body/eval_jaxpr/hqk,kv->hqv/dot_general | solution.py:43
  129.5 1.8 bitcast_reduce_fusion.2
  132.8 2.2 %fusion.102 = f32[8,256,192]{1,2,0:T(8,128)S(1)} fusion(f32[8,256,192]{1,2,0:T(8,128)S(1)} %copy-done.1, f32[512,256,8]{1,0,2:T(8,128)S(1)} %get-tuple-element.160, f32[8,256]{1,0:T(8,128)S(1)} %select_maximum_fusion.2, f32[8,256]{1,0:T(8,128)S(1)} %get-tuple-element.162, pred[]{:T(512)S(6)} %compare.44, ...), kind=kOutput, calls=%fused_computation.9.clone.1 | convolution fusion | flops 406978560 | bytes 7553029 | tf_op jit(solution)/shard_map/while/body/eval_jaxpr/hqk,kv->hqv/dot_general | solution.py:43
  136.2 1.8 bitcast_reduce_fusion.2
  139.4 2.2 %fusion.102 = f32[8,256,192]{1,2,0:T(8,128)S(1)} fusion(f32[8,256,192]{1,2,0:T(8,128)S(1)} %copy-done.1, f32[512,256,8]{1,0,2:T(8,128)S(1)} %get-tuple-element.160, f32[8,256]{1,0:T(8,128)S(1)} %select_maximum_fusion.2, f32[8,256]{1,0:T(8,128)S(1)} %get-tuple-element.162, pred[]{:T(512)S(6)} %compare.44, ...), kind=kOutput, calls=%fused_computation.9.clone.1 | convolution fusion | flops 406978560 | bytes 7553029 | tf_op jit(solution)/shard_map/while/body/eval_jaxpr/hqk,kv->hqv/dot_general | solution.py:43
  142.8 1.8 bitcast_reduce_fusion.2
  146.1 2.2 %fusion.102 = f32[8,256,192]{1,2,0:T(8,128)S(1)} fusion(f32[8,256,192]{1,2,0:T(8,128)S(1)} %copy-done.1, f32[512,256,8]{1,0,2:T(8,128)S(1)} %get-tuple-element.160, f32[8,256]{1,0:T(8,128)S(1)} %select_maximum_fusion.2, f32[8,256]{1,0:T(8,128)S(1)} %get-tuple-element.162, pred[]{:T(512)S(6)} %compare.44, ...), kind=kOutput, calls=%fused_computation.9.clone.1 | convolution fusion | flops 406978560 | bytes 7553029 | tf_op jit(solution)/shard_map/while/body/eval_jaxpr/hqk,kv->hqv/dot_general | solution.py:43
  149.5 1.8 bitcast_reduce_fusion.2
  152.7 2.2 %fusion.102 = f32[8,256,192]{1,2,0:T(8,128)S(1)} fusion(f32[8,256,192]{1,2,0:T(8,128)S(1)} %copy-done.1, f32[512,256,8]{1,0,2:T(8,128)S(1)} %get-tuple-element.160, f32[8,256]{1,0:T(8,128)S(1)} %select_maximum_fusion.2, f32[8,256]{1,0:T(8,128)S(1)} %get-tuple-element.162, pred[]{:T(512)S(6)} %compare.44, ...), kind=kOutput, calls=%fused_computation.9.clone.1 | convolution fusion | flops 406978560 | bytes 7553029 | tf_op jit(solution)/shard_map/while/body/eval_jaxpr/hqk,kv->hqv/dot_general | solution.py:43
  156.1 1.6 divide_convert_fusion
  157.7 4.8 %convert_reduce_fusion = (f32[16,1536]{1,0:T(8,128)S(1)}, bf16[256,1536]{1,0:T(8,128)(2,1)}) fusion(bf16[256,1536]{0,1:T(8,128)(2,1)S(1)} %bitcast.117, bf16[1536,1536]{1,0:T(8,128)(2,1)} %param.20, bf16[256,1536]{1,0:T(8,128)(2,1)S(1)} %copy-done.5), kind=kOutput, calls=%fused_computation.61 | convolution fusion | flops 1209901056 | bytes 7176192 | tf_op jit(solution)/shard_map/dot_general | solution.py:113
  162.9 19.5 %all_gather.11 = bf16[256,128]{1,0:T(8,128)(2,1)S(1)} all-gather(bf16[16,128]{1,0:T(8,128)(2,1)S(1)} %convolution_convert_fusion.3), channel_id=1, replica_groups=mesh['groups'=2,'seq'=16] {'seq'}, dimensions={0}, use_global_device_ids=true | all-gather | bytes 69632 | tf_op jit(solution)/shard_map/all_gather | solution.py:121
  183.3 2.3 %collective-permute-start.2 = (bf16[1,256,128]{2,1,0:T(8,128)(2,1)S(1)}, bf16[1,256,128]{2,1,0:T(8,128)(2,1)S(1)}, u32[]{:S(2)}, u32[]{:S(2)}) collective-permute-start(bf16[1,256,128]{2,1,0:T(8,128)(2,1)S(1)} %get-tuple-element.106), channel_id=1, source_target_pairs={{0,1},{1,2},{2,3},{3,4},{4,5},{5,6},{6,7},{7,8},{8,9},{9,10},{10,1... | collective-permute-start | bytes 196616 | tf_op jit(solution)/shard_map/ppermute | solution.py:18
  185.5 1.5 collective-permute-start.3
  187.0 1.7 collective-permute-done.3
  (119 shorter events, 34.3 us)
Async XLA Ops:
  7.2 16.7 %copy-start = (bf16[1536,1024]{1,0:T(8,128)(2,1)S(1)}, bf16[1536,1024]{1,0:T(8,128)(2,1)}, u32[]{:S(2)}) copy-start(bf16[1536,1024]{1,0:T(8,128)(2,1)} %param.17) | copy-start | bytes 9437188
  7.2 6.8 %copy-start.9 = (f32[5,1536]{1,0:T(8,128)S(1)}, f32[5,1536]{1,0:T(8,128)}, u32[]{:S(2)}) copy-start(f32[5,1536]{1,0:T(8,128)} %param.15) | copy-start | bytes 92164
  7.2 56.3 %all-gather.5.cloned.1.call-start = ((), (), s32[]{:S(2)}) async-start(), calls=%async_computation.1 | async-start | bytes 1671168 | tf_op jit(solution)/shard_map/all_gather | solution.py:106
  7.2 10.6 %copy-start.3 = (bf16[256,1536]{1,0:T(8,128)(2,1)S(1)}, bf16[256,1536]{1,0:T(8,128)(2,1)}, u32[]{:S(2)}) copy-start(bf16[256,1536]{1,0:T(8,128)(2,1)} %param.13) | copy-start | bytes 2359300
  8.8 11.5 %copy-start.10 = (bf16[1536,192]{0,1:T(8,128)(2,1)S(1)}, bf16[1536,192]{0,1:T(8,128)(2,1)}, u32[]{:S(2)}) copy-start(bf16[1536,192]{0,1:T(8,128)(2,1)} %param.19) | copy-start | bytes 1769476
  8.8 11.5 %copy-start.11 = (f32[1536]{0:T(1024)S(1)}, f32[1536]{0:T(1024)}, u32[]{:S(2)}) copy-start(f32[1536]{0:T(1024)} %param.16) | copy-start | bytes 18436
  10.3 3.8 %collective-permute-start = (bf16[2,1536]{1,0:T(2,128)(2,1)S(1)}, bf16[2,1536]{1,0:T(2,128)(2,1)S(1)}, u32[]{:S(2)}, u32[]{:S(2)}) collective-permute-start(bf16[2,1536]{1,0:T(2,128)(2,1)S(1)} %get-tuple-element.108), channel_id=1, source_target_pairs={{0,1},{1,2},{2,3},{3,4},{4,5},{5,6},{6,7},{7,8},{8,9},{9,10},{10,1... | collective-permute-start | bytes 18440 | tf_op jit(solution)/shard_map/ppermute | solution.py:18
  12.7 5.2 %collective-permute-start.1 = (bf16[2,1536]{1,0:T(2,128)(2,1)S(1)}, bf16[2,1536]{1,0:T(2,128)(2,1)S(1)}, u32[]{:S(2)}, u32[]{:S(2)}) collective-permute-start(bf16[2,1536]{1,0:T(2,128)(2,1)S(1)} %get-tuple-element.109), channel_id=1, source_target_pairs={{1,0},{2,1},{3,2},{4,3},{5,4},{6,5},{7,6},{8,7},{9,8},{10,9},{11,1... | collective-permute-start | bytes 18440 | tf_op jit(solution)/shard_map/ppermute | solution.py:20
  19.4 0.9 copy-start.4
  21.5 81.5 %all-gather.3.cloned.1.call-start = ((), (), s32[]{:S(2)}) async-start(), calls=%async_computation | async-start | bytes 1114112 | tf_op jit(solution)/shard_map/all_gather | solution.py:105
  104.9 1.4 copy-start.1
  108.5 1.2 copy-start.2
  111.5 1.4 copy-start.1
  115.1 1.2 copy-start.2
  118.1 1.4 copy-start.1
  121.7 1.2 copy-start.2
  124.8 1.4 copy-start.1
  128.4 1.2 copy-start.2
  131.4 1.4 copy-start.1
  135.0 1.2 copy-start.2
  138.0 1.4 copy-start.1
  141.7 1.2 copy-start.2
  144.7 1.4 copy-start.1
  148.3 1.2 copy-start.2
  151.3 1.4 copy-start.1
  154.9 1.2 copy-start.2
  156.1 1.6 copy-start.5
  157.7 4.9 %copy-start.7 = (bf16[1536,128]{1,0:T(8,128)(2,1)S(1)}, bf16[1536,128]{1,0:T(8,128)(2,1)}, u32[]{:S(2)}) copy-start(bf16[1536,128]{1,0:T(8,128)(2,1)} %param.22) | copy-start | bytes 1179652
  157.7 5.0 %copy-start.6 = (bf16[1536,128]{1,0:T(8,128)(2,1)S(1)}, bf16[1536,128]{1,0:T(8,128)(2,1)}, u32[]{:S(2)}) copy-start(bf16[1536,128]{1,0:T(8,128)(2,1)} %param.21) | copy-start | bytes 1179652
  183.3 3.7 %collective-permute-start.2 = (bf16[1,256,128]{2,1,0:T(8,128)(2,1)S(1)}, bf16[1,256,128]{2,1,0:T(8,128)(2,1)S(1)}, u32[]{:S(2)}, u32[]{:S(2)}) collective-permute-start(bf16[1,256,128]{2,1,0:T(8,128)(2,1)S(1)} %get-tuple-element.106), channel_id=1, source_target_pairs={{0,1},{1,2},{2,3},{3,4},{4,5},{5,6},{6,7},{7,8},{8,9},{9,10},{10,1... | collective-permute-start | bytes 196616 | tf_op jit(solution)/shard_map/ppermute | solution.py:18
  185.5 3.1 %collective-permute-start.3 = (bf16[1,256,128]{2,1,0:T(8,128)(2,1)S(1)}, bf16[1,256,128]{2,1,0:T(8,128)(2,1)S(1)}, u32[]{:S(2)}, u32[]{:S(2)}) collective-permute-start(bf16[1,256,128]{2,1,0:T(8,128)(2,1)S(1)} %get-tuple-element.107), channel_id=1, source_target_pairs={{1,0},{2,1},{3,2},{4,3},{5,4},{6,5},{7,6},{8,7},{9,8},{10,9},{11,1... | collective-permute-start | bytes 196616 | tf_op jit(solution)/shard_map/ppermute | solution.py:20
  189.0 1.5 copy-start.8
Sparse Core Ops, SparseCore 0:
  21.6 41.9 all-gather.4
  65.7 37.2 all-gather.2
where the time goes:
time: 206 us; the launch traced here: 203 us
  waiting for transfers between devices  78.8 us (38%)
  matrix products  46.8 us (23%)
  local copies, waits for them, and re-layouts  20.7 us (10%)
  blocking collectives  19.5 us (9%)
  between operations  14.4 us (7%)
  other arithmetic  14.3 us (7%)
  starting transfers between devices  7.49 us (4%)
    all_gather x1, waiting for transfers between devices, local(): lax.all_gather(keys_local, 'seq', axis=0, tiled=True)  36.7 us
    all_gather x1, waiting for transfers between devices, local(): lax.all_gather(values_local, 'seq', axis=0, tiled=True)  36.6 us
    all_gather x1, blocking collectives, local(): right_all = lax.all_gather(right, 'seq', axis=0, tiled=True)  19.5 us
    dot_general x8, matrix products, attend_block(): jnp.einsum('hqk,kv->hqv', expo.astype(jnp.bfloat16), values_part, preferr...  17.7 us
    dot_general x8, matrix products, attend_block(): jnp.einsum('qhd,kd->hqk', queries, keys_part, preferred_element_type=jnp....  14.6 us
    while x40, local copies, waits for them, and re-layouts  14.6 us
    reduce_sum x8, other arithmetic, attend_block(): totals = totals * factor + jnp.sum(expo, axis=-1)  5.56 us
    ppermute x2, waiting for transfers between devices, extended_2(): lax.ppermute(head, axis, [((i + 1) % count, i) for i in range(ends)])  5.43 us
  transfers between devices with their start and end apart: 6, of which 4 were waited for; matrix products, arithmetic and copies ran while one was open for 4% of the time, Pallas kernels for 0%

commit v1 on v0

v1 whole, which is shorter than its diff:
```python
import functools
import math

import jax
import jax.numpy as jnp
from jax import lax
from jax.experimental import pallas as pl
from jax.experimental.pallas import tpu as pltpu
from jax.sharding import PartitionSpec as P

HEADS = 8
POOL = 16
HALO = 16
PARTS = 2
F32 = jnp.float32
BF16 = jnp.bfloat16


def dot(a, b):
    return jnp.dot(a, b, preferred_element_type=F32)


def dot_t(a, b):
    return lax.dot_general(a, b, (((1,), (1,)), ((), ())), preferred_element_type=F32)


def rms_norm(values, gain):
    scale = lax.rsqrt(jnp.mean(values * values, axis=-1, keepdims=True) + 1e-06)
    return values * scale * gain


def kernel(
    n,
    seq_ref, gconv_ref, conv_ref, gattn_ref,
    wq_hbm, wk_hbm, wv_hbm, wo_hbm, wl_hbm, wr_hbm, wp_hbm,
    track_ref, pair_ref,
    wq, wk, wv, wo, wl, wr, wp,
    halo, padded, first, attn, q_ref, kv, acc, top, attended,
    own_left, left_halo, left_ext, right_land, right_all, act,
    w_sem, halo_send, halo_recv, r_send, l_send, p_send, kv_recv,
    left_send, left_recv, right_send, right_recv,
):
    rows, width = seq_ref.shape
    key = wk.shape[1]
    val = wv.shape[1]
    taps = conv_ref.shape[0]
    reach = taps // 2
    part = rows // PARTS
    chips = n // 2
    half = (chips + 1) // 2
    me = lax.axis_index("seq")
    chip = me // 2
    core = me % 2
    partner = chip * 2 + (1 - core)
    pos = jnp.where(chip % 2 == 0, chip // 2, chips - 1 - chip // 2)

    def chip_at(place):
        place = lax.rem(place + 2 * chips, chips)
        return jnp.where(place < half, 2 * place, 2 * (chips - 1 - place) + 1)

    def mine_at(place):
        return chip_at(place) * 2 + core

    def other_at(place):
        return chip_at(place) * 2 + (1 - core)

    barrier = pltpu.get_barrier_semaphore()

    @pl.loop(1, n)
    def _(step):
        pl.semaphore_signal(barrier, inc=1, device_id={"seq": lax.rem(me + step, n)})

    pairs = ((wk_hbm, wk), (wv_hbm, wv), (wq_hbm, wq), (wo_hbm, wo), (wl_hbm, wl), (wr_hbm, wr), (wp_hbm, wp))
    loads = [pltpu.make_async_copy(s, d, w_sem.at[i]) for i, (s, d) in enumerate(pairs)]
    for load in loads:
        load.start()
    pl.semaphore_wait(barrier, n - 1)

    def send(src, dst, ssem, rsem, to):
        return pltpu.make_async_remote_copy(
            src_ref=src, dst_ref=dst, send_sem=ssem, recv_sem=rsem, device_id={"seq": to}
        )

    has_prev = me > 0
    has_next = me < n - 1
    prev = lax.rem(me + n - 1, n)
    after = lax.rem(me + 1, n)
    to_next = send(seq_ref.at[pl.ds(rows - HALO, HALO)], halo.at[0], halo_send.at[0], halo_recv.at[0], after)
    to_prev = send(seq_ref.at[pl.ds(0, HALO)], halo.at[1], halo_send.at[1], halo_recv.at[1], prev)

    @pl.when(has_next)
    def _():
        to_next.start()

    @pl.when(has_prev)
    def _():
        to_prev.start()

    gconv = gconv_ref[...]
    strip = 32
    for start in range(0, rows, strip):
        values = seq_ref[start:start + strip, :].astype(F32)
        padded[HALO + start:HALO + start + strip, :] = rms_norm(values, gconv).astype(BF16).astype(F32)

    @pl.when(has_prev)
    def _():
        to_next.wait_recv()
        padded[0:HALO, :] = rms_norm(halo[0].astype(F32), gconv).astype(BF16).astype(F32)

    @pl.when(jnp.logical_not(has_prev))
    def _():
        padded[0:HALO, :] = jnp.zeros((HALO, width), F32)

    @pl.when(has_next)
    def _():
        to_prev.wait_recv()
        padded[HALO + rows:, :] = rms_norm(halo[1].astype(F32), gconv).astype(BF16).astype(F32)

    @pl.when(jnp.logical_not(has_next))
    def _():
        padded[HALO + rows:, :] = jnp.zeros((HALO, width), F32)

    gattn = gattn_ref[...]
    for start in range(0, rows, strip):
        total = seq_ref[start:start + strip, :].astype(F32)
        conv = jnp.zeros((strip, width), F32)
        for tap in range(taps):
            base = HALO + start + tap - reach
            conv = conv + conv_ref[tap:tap + 1, :] * padded[base:base + strip, :]
        one = (total + conv).astype(BF16)
        first[start:start + strip, :] = one
        attn[start:start + strip, :] = rms_norm(one.astype(F32), gattn).astype(BF16)

    loads[0].wait()
    loads[1].wait()
    kv[me, :, 0:key] = dot(attn[...], wk[...]).astype(BF16)
    kv[me, :, key:key + val] = dot(attn[...], wv[...]).astype(BF16)
    kv[me, :, key + val:] = jnp.ones((rows, kv.shape[2] - key - val), BF16)

    right_steps = chips // 2
    left_steps = chips - 1 - right_steps
    to_right = mine_at(pos + 1)
    to_left = mine_at(pos - 1)

    def piece(slot, c):
        return kv.at[slot, pl.ds(c * part, part)]

    def copy_right(t, c):
        slot = mine_at(pos - t)
        return send(piece(slot, c), piece(slot, c), r_send.at[t, c], kv_recv.at[slot, c], to_right)

    def copy_left(t, c):
        slot = mine_at(pos + t)
        return send(piece(slot, c), piece(slot, c), l_send.at[t, c], kv_recv.at[slot, c], to_left)

    def copy_partner(slot, count, c):
        return send(piece(slot, c), piece(slot, c), p_send.at[count, c], kv_recv.at[slot, c], partner)

    def arrived(slot, c):
        send(piece(slot, c), piece(slot, c), p_send.at[0, c], kv_recv.at[slot, c], partner).wait_recv()

    sent = []

    def go(copy):
        copy.start()
        sent.append(copy)

    for c in range(PARTS):
        if right_steps:
            go(copy_right(0, c))
        if left_steps:
            go(copy_left(0, c))
        go(copy_partner(me, 0, c))

    loads[2].wait()
    scale = math.log2(math.e) / math.sqrt(key)
    for h in range(HEADS):
        q_ref[h] = (dot(attn[...], wq[:, h * key:(h + 1) * key]) * scale).astype(BF16)

    def attend(pieces, initial):
        keys = jnp.concatenate([kv[s, c * part:(c + 1) * part, 0:key] for s, c in pieces], axis=0)
        values = jnp.concatenate([kv[s, c * part:(c + 1) * part, key:] for s, c in pieces], axis=0)
        wide = keys.shape[0] // 128

        @pl.loop(0, HEADS, unroll=2)
        def _(h):
            scores = dot_t(q_ref[h], keys)
            best = jnp.broadcast_to(jnp.max(scores, axis=1, keepdims=True), (rows, 128))
            if not initial:
                old = top[h]
                best = jnp.maximum(old, best)
            weights = jnp.exp2(scores - jnp.concatenate([best] * wide, axis=1)).astype(BF16)
            update = dot(weights, values)
            if initial:
                acc[h] = update
            else:
                factor = jnp.exp2(old - best)
                acc[h] = acc[h] * jnp.concatenate([factor] * (update.shape[1] // 128), axis=1) + update
            top[h] = best

    for c in range(PARTS):
        arrived(partner, c)
    attend([(s, c) for s in (me, partner) for c in range(PARTS)], True)

    waiting = None
    count = 1
    for t in range(right_steps):
        both = t < left_steps
        slots = [pos - 1 - t] + ([pos + 1 + t] if both else [])
        for c in range(PARTS):
            for k, place in enumerate(slots):
                slot = mine_at(place)
                arrived(slot, c)
                if k == 0 and t + 1 < right_steps:
                    go(copy_right(t + 1, c))
                if k == 1 and t + 1 < left_steps:
                    go(copy_left(t + 1, c))
                go(copy_partner(slot, count + k, c))
            if waiting is not None:
                for s, cc in waiting[1]:
                    arrived(s, cc)
                attend(waiting[0] + waiting[1], False)
            waiting = ([(mine_at(p), c) for p in slots], [(other_at(p), c) for p in slots])
        count += len(slots)
    if waiting is not None:
        for s, cc in waiting[1]:
            arrived(s, cc)
        attend(waiting[0] + waiting[1], False)

    for pair in range(0, HEADS, 2):
        both = []
        for h in (pair, pair + 1):
            block = acc[h]
            both.append((block[:, :val] / block[:, val:val + 1]).astype(BF16))
        attended[:, pair * val:(pair + 2) * val] = jnp.concatenate(both, axis=1)

    loads[3].wait()
    band = rows // POOL
    member = lax.broadcasted_iota(jnp.int32, (band, rows), 1) // POOL
    pool = jnp.where(member == lax.broadcasted_iota(jnp.int32, (band, rows), 0), 1.0 / POOL, 0.0).astype(BF16)
    loads[4].wait()
    loads[5].wait()
    left = jnp.zeros((band, wl.shape[1]), F32)
    right = jnp.zeros((band, wr.shape[1]), F32)
    cols = 512 if width % 512 == 0 else width
    for start in range(0, width, cols):
        stop = start + cols
        block = (first[:, start:stop].astype(F32) + dot(attended[...], wo[:, start:stop])).astype(BF16)
        track_ref[:, start:stop] = block
        pooled = dot(pool, block).astype(BF16)
        left = left + dot(pooled, wl[start:stop, :])
        right = right + dot(pooled, wr[start:stop, :])
    own_left[...] = left.astype(BF16)
    right_land[me] = right.astype(BF16)

    left_next = send(own_left, left_halo.at[0], left_send.at[0], left_recv.at[0], after)
    left_prev = send(own_left, left_halo.at[1], left_send.at[1], left_recv.at[1], prev)

    @pl.when(has_next)
    def _():
        left_next.start()

    @pl.when(has_prev)
    def _():
        left_prev.start()

    def right_copy(step):
        return send(right_land.at[me], right_land.at[me], right_send.at[step], right_recv.at[me], lax.rem(me + step, n))

    @pl.loop(1, n)
    def _(step):
        right_copy(step).start()

    left_ext[...] = jnp.zeros(left_ext.shape, F32)
    left_ext[8:8 + band, :] = own_left[...].astype(F32)

    @pl.when(has_prev)
    def _():
        left_next.wait_recv()
        left_ext[7:8, :] = left_halo[0].astype(F32)[band - 1:band, :]

    @pl.when(has_next)
    def _():
        left_prev.wait_recv()
        left_ext[8 + band:9 + band, :] = left_halo[1].astype(F32)[0:1, :]

    @pl.loop(1, n)
    def _(step):
        slot = lax.rem(me + step, n)
        send(right_land.at[slot], right_land.at[slot], right_send.at[step], right_recv.at[slot], slot).wait_recv()

    columns = n * band
    right_all[...] = right_land[...].astype(F32).reshape(columns, right_all.shape[1])
    loads[6].wait()
    channels = right_all.shape[1]
    column = lax.broadcasted_iota(jnp.int32, (columns, channels), 0)

    @pl.loop(0, band + 2)
    def _(i):
        product = (left_ext[pl.ds(i + 7, 1), :] * right_all[...]).astype(BF16).astype(F32)
        active = jax.nn.gelu(product)
        act[i, :, 0:channels] = jnp.where(column == 0, 0.0, pltpu.roll(active, 1, 0)).astype(BF16)
        act[i, :, channels:2 * channels] = active.astype(BF16)
        act[i, :, 2 * channels:] = jnp.where(column == columns - 1, 0.0, pltpu.roll(active, columns - 1, 0)).astype(BF16)

    span = 3 * channels

    @pl.loop(0, band)
    def _(i):
        total = (left_ext[pl.ds(i + 8, 1), :] * right_all[...]).astype(BF16).astype(F32)
        for a in range(3):
            total = total + dot(act[i + a], wp[a * span:(a + 1) * span, :])
        pair_ref[i] = total.astype(BF16)

    @pl.when(has_next)
    def _():
        to_next.wait_send()
        left_next.wait_send()

    @pl.when(has_prev)
    def _():
        to_prev.wait_send()
        left_prev.wait_send()

    for copy in sent:
        copy.wait_send()

    @pl.loop(1, n)
    def _(step):
        right_copy(step).wait_send()


def solution(mesh):
    n = mesh.shape["seq"]

    def local(sequence, gain_conv, conv_weight, gain_attn, w_query, w_key, w_value, w_out, w_left, w_right, w_pair):
        rows, width = sequence.shape
        key, val = w_key.shape[1], w_value.shape[1]
        channels = w_left.shape[1]
        band = rows // POOL
        columns = n * band
        chips = n // 2
        value_lanes = (val // 128 + 1) * 128
        taps = w_pair.reshape(-1, channels)
        weights = (w_query, w_key, w_value, w_out, w_left, w_right, taps)
        vmem = pl.BlockSpec(memory_space=pltpu.VMEM)
        dma = pltpu.SemaphoreType.DMA
        steps = max(chips // 2, 1)
        return pl.pallas_call(
            functools.partial(kernel, n),
            out_shape=(
                jax.ShapeDtypeStruct((rows, width), BF16),
                jax.ShapeDtypeStruct((band, columns, channels), BF16),
            ),
            in_specs=[vmem] * 4 + [pl.BlockSpec(memory_space=pl.ANY)] * 7,
            out_specs=(vmem, vmem),
            scratch_shapes=[pltpu.VMEM(w.shape, BF16) for w in weights]
            + [
                pltpu.VMEM((2, HALO, width), BF16),
                pltpu.VMEM((rows + 2 * HALO, width), F32),
                pltpu.VMEM((rows, width), BF16),
                pltpu.VMEM((rows, width), BF16),
                pltpu.VMEM((HEADS, rows, key), BF16),
                pltpu.VMEM((n, rows, key + value_lanes), BF16),
                pltpu.VMEM((HEADS, rows, value_lanes), F32),
                pltpu.VMEM((HEADS, rows, 128), F32),
                pltpu.VMEM((rows, HEADS * val), BF16),
                pltpu.VMEM((band, channels), BF16),
                pltpu.VMEM((2, band, channels), BF16),
                pltpu.VMEM((band + 16, channels), F32),
                pltpu.VMEM((n, band, channels), BF16),
                pltpu.VMEM((columns, channels), F32),
                pltpu.VMEM((band + 2, columns, 3 * channels), BF16),
                dma((len(weights),)),
                dma((2,)),
                dma((2,)),
                dma((steps, PARTS)),
                dma((steps, PARTS)),
                dma((chips, PARTS)),
                dma((n, PARTS)),
                dma((2,)),
                dma((2,)),
                dma((n,)),
                dma((n,)),
            ],
            compiler_params=pltpu.CompilerParams(
                collective_id=0, has_side_effects=True, vmem_limit_bytes=60 * 1024 * 1024
            ),
        )(sequence, gain_conv.reshape(1, -1), conv_weight, gain_attn.reshape(1, -1), *weights)

    placed = (P(("groups", "seq"), None),) + (P(),) * 10
    return jax.shard_map(
        local,
        mesh=mesh,
        in_specs=placed,
        out_specs=(P(("groups", "seq"), None), P(("groups", "seq"), None, None)),
        check_vma=False,
    )
```

time: 206 us -> 65.3 us (0.32); the launches traced: 203 us -> 64.9 us
  waiting for transfers between devices: 78.8 us -> 0 us
  Pallas kernels: 0 us -> 55.1 us
  matrix products: 46.8 us -> 0 us
  blocking collectives: 19.5 us -> 0 us
  other arithmetic: 14.3 us -> 0 us
  between operations: 14.4 us -> 0.64 us
  local copies, waits for them, and re-layouts: 20.7 us -> 9.17 us
  starting transfers between devices: 7.49 us -> 0 us
    all_gather x2 -> x0, waiting for transfers between devices: 73.3 us -> none  [the longest x1 36.7 us: local(): lax.all_gather(keys_local, 'seq', axis=0, tiled=True)]
    pallas_call x0 -> x1, Pallas kernels: none -> 55.1 us  [local(): pl.pallas_call(functools.partial(kernel, n), out_shape=(jax.ShapeDtypeStr...]
    dot_general x31 -> x0, matrix products: 46.8 us -> none  [the longest x8 17.7 us: attend_block(): jnp.einsum('hqk,kv->hqv', expo.astype(jnp.bfloat16), values_part, preferr...]
    all_gather x1 -> x0, blocking collectives: 19.5 us -> none  [local(): right_all = lax.all_gather(right, 'seq', axis=0, tiled=True)]
    while x40 -> x0, local copies, waits for them, and re-layouts: 14.6 us -> none
    reduce_sum x10 -> x0, other arithmetic: 8.63 us -> none  [the longest x8 5.56 us: attend_block(): totals = totals * factor + jnp.sum(expo, axis=-1)]
    ppermute x4 -> x0, starting transfers between devices: 7.41 us -> none  [the longest x2 4.65 us: extended_2(): lax.ppermute(tail, axis, [(i, (i + 1) % count) for i in range(ends)])]
    unnamed x20 -> x3, local copies, waits for them, and re-layouts: 0.91 us -> 6.57 us
  transfers between devices with their start and end apart: 6 -> 0, of which waited for: 4 -> 0; matrix products, arithmetic and copies ran while one was open for 4% -> 0% of each run, Pallas kernels for 0% -> 0%
where the time goes in v1:
time: 65.3 us; the launch traced here: 64.9 us
  Pallas kernels  55.1 us (84%)
  local copies, waits for them, and re-layouts  9.17 us (14%)
    pallas_call x1, Pallas kernels, local(): pl.pallas_call(functools.partial(kernel, n), out_shape=(jax.ShapeDtypeStr...  55.1 us
    unnamed x3, local copies, waits for them, and re-layouts  6.57 us

profile of v1, /device:TPU:0, one launch (start us, length us, event | category | flops | bytes accessed | tf_op | source)
XLA Modules:
  0.0 64.9 jit_solution(15403904974150394876)
XLA Ops:
  0.6 1.3 %reshape.13.gconv_ref = f32[1,1536]{1,0:T(1,128)} reshape(f32[1536]{0:T(1024)} %param.12) | data formatting | bytes 12288 | tf_op jit(solution)/shard_map/reshape | solution.py:389
  1.9 1.3 %reshape.14.gattn_ref = f32[1,1536]{1,0:T(1,128)} reshape(f32[1536]{0:T(1024)} %param.14) | data formatting | bytes 12288 | tf_op jit(solution)/shard_map/reshape | solution.py:389
  3.2 2.2 %copy.13.wv_hbm = bf16[1536,192]{1,0:T(8,128)(2,1)} copy(bf16[1536,192]{0,1:T(8,128)(2,1)} %param.17) | data formatting | bytes 1179648 | tf_op args[6]
  5.4 55.1 %shard_map.122 = (bf16[256,1536]{1,0:T(8,128)(2,1)}, bf16[16,256,128]{2,1,0:T(8,128)(2,1)}) custom-call(bf16[256,1536]{1,0:T(8,128)(2,1)} %seq_ref.1, f32[1,1536]{1,0:T(1,128)} %reshape.13.gconv_ref, f32[5,1536]{1,0:T(8,128)} %conv_ref.1, f32[1,1536]{1,0:T(1,128)} %reshape.14.gattn_ref, bf16[1536,1024]{1,0:T(8,128)(2,1)} %wq_hbm.1, ...), custom_call_target="tpu_custom_call" | custom-call | tf_op jit(solution)/shard_map/pallas_call | solution.py:349
  60.6 2.1 %copy.16 = bf16[256,1536]{1,0:T(8,128)(2,1)} copy(bf16[256,1536]{1,0:T(8,128)(2,1)} %get-tuple-element.4) | data formatting | bytes 1572864
  62.6 2.3 %copy.17 = bf16[16,256,128]{2,1,0:T(8,128)(2,1)} copy(bf16[16,256,128]{2,1,0:T(8,128)(2,1)} %get-tuple-element.5) | data formatting | bytes 2097152

commit v2 on v1

--- a/solution.py
+++ b/solution.py
@@ -31,18 +31,18 @@
 
 def kernel(
     n,
-    seq_ref, gconv_ref, conv_ref, gattn_ref,
-    wq_hbm, wk_hbm, wv_hbm, wo_hbm, wl_hbm, wr_hbm, wp_hbm,
-    track_ref, pair_ref,
-    wq, wk, wv, wo, wl, wr, wp,
+    seq_ref, conv_ref,
+    gconv_hbm, gattn_hbm, wq_hbm, wk_hbm, wv_hbm, wo_hbm, wl_hbm, wr_hbm,
+    track_hbm, left_ext, right_land,
+    gains, wq, wk, wv, wo, wl, wr, track_ref,
     halo, padded, first, attn, q_ref, kv, acc, top, attended,
-    own_left, left_halo, left_ext, right_land, right_all, act,
-    w_sem, halo_send, halo_recv, r_send, l_send, p_send, kv_recv,
+    own_left, left_halo,
+    w_sem, track_sem, halo_send, halo_recv, r_send, l_send, p_send, kv_recv,
     left_send, left_recv, right_send, right_recv,
 ):
     rows, width = seq_ref.shape
     key = wk.shape[1]
-    val = wv.shape[1]
+    val = wv.shape[0]
     taps = conv_ref.shape[0]
     reach = taps // 2
     part = rows // PARTS
@@ -70,9 +70,12 @@
     def _(step):
         pl.semaphore_signal(barrier, inc=1, device_id={"seq": lax.rem(me + step, n)})
 
-    pairs = ((wk_hbm, wk), (wv_hbm, wv), (wq_hbm, wq), (wo_hbm, wo), (wl_hbm, wl), (wr_hbm, wr), (wp_hbm, wp))
+    pairs = (
+        (wk_hbm, wk), (wv_hbm, wv), (wq_hbm, wq), (wo_hbm, wo), (wl_hbm, wl), (wr_hbm, wr),
+        (gconv_hbm, gains.at[0]), (gattn_hbm, gains.at[1]),
+    )
     loads = [pltpu.make_async_copy(s, d, w_sem.at[i]) for i, (s, d) in enumerate(pairs)]
-    for load in loads:
+    for load in loads[6:] + loads[:6]:
         load.start()
     pl.semaphore_wait(barrier, n - 1)
 
@@ -96,7 +99,9 @@
     def _():
         to_prev.start()
 
-    gconv = gconv_ref[...]
+    loads[6].wait()
+    loads[7].wait()
+    gconv = gains[0:1, :]
     strip = 32
     for start in range(0, rows, strip):
         values = seq_ref[start:start + strip, :].astype(F32)
@@ -120,7 +125,7 @@
     def _():
         padded[HALO + rows:, :] = jnp.zeros((HALO, width), F32)
 
-    gattn = gattn_ref[...]
+    gattn = gains[1:2, :]
     for start in range(0, rows, strip):
         total = seq_ref[start:start + strip, :].astype(F32)
         conv = jnp.zeros((strip, width), F32)
@@ -134,7 +139,7 @@
     loads[0].wait()
     loads[1].wait()
     kv[me, :, 0:key] = dot(attn[...], wk[...]).astype(BF16)
-    kv[me, :, key:key + val] = dot(attn[...], wv[...]).astype(BF16)
+    kv[me, :, key:key + val] = dot_t(attn[...], wv[...]).astype(BF16)
     kv[me, :, key + val:] = jnp.ones((rows, kv.shape[2] - key - val), BF16)
 
     right_steps = chips // 2
@@ -250,6 +255,8 @@
         pooled = dot(pool, block).astype(BF16)
         left = left + dot(pooled, wl[start:stop, :])
         right = right + dot(pooled, wr[start:stop, :])
+    track_out = pltpu.make_async_copy(track_ref, track_hbm, track_sem)
+    track_out.start()
     own_left[...] = left.astype(BF16)
     right_land[me] = right.astype(BF16)
 
@@ -289,10 +296,37 @@
         slot = lax.rem(me + step, n)
         send(right_land.at[slot], right_land.at[slot], right_send.at[step], right_recv.at[slot], slot).wait_recv()
 
-    columns = n * band
-    right_all[...] = right_land[...].astype(F32).reshape(columns, right_all.shape[1])
-    loads[6].wait()
-    channels = right_all.shape[1]
+    @pl.when(has_next)
+    def _():
+        to_next.wait_send()
+        left_next.wait_send()
+
+    @pl.when(has_prev)
+    def _():
+        to_prev.wait_send()
+        left_prev.wait_send()
+
+    for copy in sent:
+        copy.wait_send()
+
+    @pl.loop(1, n)
+    def _(step):
+        right_copy(step).wait_send()
+
+    track_out.wait()
+
+
+def pair_kernel(
+    track_in, left_ext, right_land, wp_hbm, track_out, pair_out,
+    track, wp, right_all, act, pair, w_sem, track_sem, pair_sem,
+):
+    load = pltpu.make_async_copy(wp_hbm, wp, w_sem)
+    load.start()
+    track_load = pltpu.make_async_copy(track_in, track, track_sem)
+    track_load.start()
+    columns, channels = right_all.shape
+    band = pair.shape[0]
+    right_all[...] = right_land[...].astype(F32).reshape(columns, channels)
     column = lax.broadcasted_iota(jnp.int32, (columns, channels), 0)
 
     @pl.loop(0, band + 2)
@@ -304,30 +338,27 @@
         act[i, :, 2 * channels:] = jnp.where(column == columns - 1, 0.0, pltpu.roll(active, columns - 1, 0)).astype(BF16)
 
     span = 3 * channels
+    track_load.wait()
+    track_store = pltpu.make_async_copy(track, track_out, track_sem)
+    track_store.start()
+    load.wait()
+
+    def store(i):
+        return pltpu.make_async_copy(pair.at[i], pair_out.at[i], pair_sem.at[i])
 
     @pl.loop(0, band)
     def _(i):
         total = (left_ext[pl.ds(i + 8, 1), :] * right_all[...]).astype(BF16).astype(F32)
         for a in range(3):
             total = total + dot(act[i + a], wp[a * span:(a + 1) * span, :])
-        pair_ref[i] = total.astype(BF16)
-
-    @pl.when(has_next)
-    def _():
-        to_next.wait_send()
-        left_next.wait_send()
-
-    @pl.when(has_prev)
-    def _():
-        to_prev.wait_send()
-        left_prev.wait_send()
-
-    for copy in sent:
-        copy.wait_send()
-
-    @pl.loop(1, n)
-    def _(step):
-        right_copy(step).wait_send()
+        pair[i] = total.astype(BF16)
+        store(i).start()
+
+    track_store.wait()
+
+    @pl.loop(0, band)
+    def _(i):
+        store(i).wait()
 
 
 def solution(mesh):
@@ -342,20 +373,24 @@
         chips = n // 2
         value_lanes = (val // 128 + 1) * 128
         taps = w_pair.reshape(-1, channels)
-        weights = (w_query, w_key, w_value, w_out, w_left, w_right, taps)
+        weights = (w_query, w_key, w_value.T, w_out, w_left, w_right)
+        anyspace = pl.BlockSpec(memory_space=pl.ANY)
         vmem = pl.BlockSpec(memory_space=pltpu.VMEM)
         dma = pltpu.SemaphoreType.DMA
         steps = max(chips // 2, 1)
-        return pl.pallas_call(
+        track, left, right = pl.pallas_call(
             functools.partial(kernel, n),
             out_shape=(
                 jax.ShapeDtypeStruct((rows, width), BF16),
-                jax.ShapeDtypeStruct((band, columns, channels), BF16),
+                jax.ShapeDtypeStruct((band + 16, channels), F32),
+                jax.ShapeDtypeStruct((n, band, channels), BF16),
             ),
-            in_specs=[vmem] * 4 + [pl.BlockSpec(memory_space=pl.ANY)] * 7,
-            out_specs=(vmem, vmem),
-            scratch_shapes=[pltpu.VMEM(w.shape, BF16) for w in weights]
+            in_specs=[vmem] * 2 + [anyspace] * 8,
+            out_specs=(anyspace, vmem, vmem),
+            scratch_shapes=[pltpu.VMEM((2, width), F32)]
+            + [pltpu.VMEM(w.shape, BF16) for w in weights]
             + [
+                pltpu.VMEM((rows, width), BF16),
                 pltpu.VMEM((2, HALO, width), BF16),
                 pltpu.VMEM((rows + 2 * HALO, width), F32),
                 pltpu.VMEM((rows, width), BF16),
@@ -367,11 +402,8 @@
                 pltpu.VMEM((rows, HEADS * val), BF16),
                 pltpu.VMEM((band, channels), BF16),
                 pltpu.VMEM((2, band, channels), BF16),
-                pltpu.VMEM((band + 16, channels), F32),
-                pltpu.VMEM((n, band, channels), BF16),
-                pltpu.VMEM((columns, channels), F32),
-                pltpu.VMEM((band + 2, columns, 3 * channels), BF16),
-                dma((len(weights),)),
+                dma((len(weights) + 2,)),
+                dma(()),
                 dma((2,)),
                 dma((2,)),
                 dma((steps, PARTS)),
@@ -386,7 +418,27 @@
             compiler_params=pltpu.CompilerParams(
                 collective_id=0, has_side_effects=True, vmem_limit_bytes=60 * 1024 * 1024
             ),
-        )(sequence, gain_conv.reshape(1, -1), conv_weight, gain_attn.reshape(1, -1), *weights)
+        )(sequence, conv_weight, gain_conv, gain_attn, *weights)
+        return pl.pallas_call(
+            pair_kernel,
+            out_shape=(
+                jax.ShapeDtypeStruct((rows, width), BF16),
+                jax.ShapeDtypeStruct((band, columns, channels), BF16),
+            ),
+            in_specs=[anyspace, vmem, vmem, anyspace],
+            out_specs=(anyspace, anyspace),
+            scratch_shapes=[
+                pltpu.VMEM((rows, width), BF16),
+                pltpu.VMEM(taps.shape, BF16),
+                pltpu.VMEM((columns, channels), F32),
+                pltpu.VMEM((band + 2, columns, 3 * channels), BF16),
+                pltpu.VMEM((band, columns, channels), BF16),
+                dma(()),
+                dma(()),
+                dma((band,)),
+            ],
+            compiler_params=pltpu.CompilerParams(vmem_limit_bytes=60 * 1024 * 1024),
+        )(track, left, right, taps)
 
     placed = (P(("groups", "seq"), None),) + (P(),) * 10
     return jax.shard_map(

time: 65.3 us -> 57.3 us (0.88)
  local copies, waits for them, and re-layouts: 9.17 us -> 0 us
  Pallas kernels: 55.1 us -> 56.4 us
    pallas_call x0 -> x1, Pallas kernels: none -> 8.08 us  [local(): pl.pallas_call(pair_kernel, out_shape=(jax.ShapeDtypeStruct((rows, width)...]
    pallas_call x1, Pallas kernels: 55.1 us -> 48.4 us  [local(): pl.pallas_call(functools.partial(kernel, n), out_shape=(jax.ShapeDtypeStr...]
    unnamed x3 -> x0, local copies, waits for them, and re-layouts: 6.57 us -> none
    reshape x2 -> x0, local copies, waits for them, and re-layouts: 2.59 us -> none  [the longest x1 1.3 us: local(): gain_attn.reshape(1, -1)]
where the time goes in v2:
time: 57.3 us; the launch traced here: 57.1 us
  Pallas kernels  56.4 us (98%)
  between operations  0.64 us (1%)
    pallas_call x1, Pallas kernels, local(): pl.pallas_call(functools.partial(kernel, n), out_shape=(jax.ShapeDtypeStr...  48.4 us
    pallas_call x1, Pallas kernels, local(): pl.pallas_call(pair_kernel, out_shape=(jax.ShapeDtypeStruct((rows, width)...  8.08 us

profile of v2, /device:TPU:0, one launch (start us, length us, event | category | flops | bytes accessed | tf_op | source)
XLA Modules:
  0.0 57.1 jit_solution(11343226563150861464)
XLA Ops:
  0.6 48.4 %shard_map.122 = (bf16[256,1536]{1,0:T(8,128)(2,1)}, f32[32,128]{1,0:T(8,128)}, bf16[16,16,128]{2,1,0:T(8,128)(2,1)}) custom-call(bf16[256,1536]{1,0:T(8,128)(2,1)} %seq_ref.1, f32[5,1536]{1,0:T(8,128)} %conv_ref.1, f32[1536]{0:T(1024)} %gconv_hbm.1, f32[1536]{0:T(1024)} %gattn_hbm.1, bf16[1536,1024]{1,0:T(8,128)(2,1)} %wq_hbm.1, bf16[1536,128]{1,0:T(8,128)(2,1)} %wk_hbm.1, ...), custom_call_target="tpu_custom_call" | custom-call | tf_op jit(solution)/shard_map/pallas_call | solution.py:381
  49.0 8.1 %shard_map.123 = (bf16[256,1536]{1,0:T(8,128)(2,1)}, bf16[16,256,128]{2,1,0:T(8,128)(2,1)}) custom-call(bf16[256,1536]{1,0:T(8,128)(2,1)} %get-tuple-element.5.track_in, f32[32,128]{1,0:T(8,128)} %get-tuple-element.6.left_ext, bf16[16,16,128]{2,1,0:T(8,128)(2,1)} %get-tuple-element.7.right_land, bf16[1152,128]{1,0:T(8,128)(2,1)} %bitcast.3), custom_call_target="tpu_custom_call" | custom-call | tf_op jit(solution)/shard_map/pallas_call | solution.py:422

commit v3 on v2

--- a/solution.py
+++ b/solution.py
@@ -36,7 +36,7 @@
     track_hbm, left_ext, right_land,
     gains, wq, wk, wv, wo, wl, wr, track_ref,
     halo, padded, first, attn, q_ref, kv, acc, top, attended,
-    own_left, left_halo,
+    own_left, left_halo, turned, stage,
     w_sem, track_sem, halo_send, halo_recv, r_send, l_send, p_send, kv_recv,
     left_send, left_recv, right_send, right_recv,
 ):
@@ -77,7 +77,6 @@
     loads = [pltpu.make_async_copy(s, d, w_sem.at[i]) for i, (s, d) in enumerate(pairs)]
     for load in loads[6:] + loads[:6]:
         load.start()
-    pl.semaphore_wait(barrier, n - 1)
 
     def send(src, dst, ssem, rsem, to):
         return pltpu.make_async_remote_copy(
@@ -90,14 +89,6 @@
     after = lax.rem(me + 1, n)
     to_next = send(seq_ref.at[pl.ds(rows - HALO, HALO)], halo.at[0], halo_send.at[0], halo_recv.at[0], after)
     to_prev = send(seq_ref.at[pl.ds(0, HALO)], halo.at[1], halo_send.at[1], halo_recv.at[1], prev)
-
-    @pl.when(has_next)
-    def _():
-        to_next.start()
-
-    @pl.when(has_prev)
-    def _():
-        to_prev.start()
 
     loads[6].wait()
     loads[7].wait()
@@ -107,26 +98,18 @@
         values = seq_ref[start:start + strip, :].astype(F32)
         padded[HALO + start:HALO + start + strip, :] = rms_norm(values, gconv).astype(BF16).astype(F32)
 
+    pl.semaphore_wait(barrier, n - 1)
+
+    @pl.when(has_next)
+    def _():
+        to_next.start()
+
     @pl.when(has_prev)
     def _():
-        to_next.wait_recv()
-        padded[0:HALO, :] = rms_norm(halo[0].astype(F32), gconv).astype(BF16).astype(F32)
-
-    @pl.when(jnp.logical_not(has_prev))
-    def _():
-        padded[0:HALO, :] = jnp.zeros((HALO, width), F32)
-
-    @pl.when(has_next)
-    def _():
-        to_prev.wait_recv()
-        padded[HALO + rows:, :] = rms_norm(halo[1].astype(F32), gconv).astype(BF16).astype(F32)
-
-    @pl.when(jnp.logical_not(has_next))
-    def _():
-        padded[HALO + rows:, :] = jnp.zeros((HALO, width), F32)
+        to_prev.start()
 
     gattn = gains[1:2, :]
-    for start in range(0, rows, strip):
+    def mix(start):
         total = seq_ref[start:start + strip, :].astype(F32)
         conv = jnp.zeros((strip, width), F32)
         for tap in range(taps):
@@ -136,6 +119,31 @@
         first[start:start + strip, :] = one
         attn[start:start + strip, :] = rms_norm(one.astype(F32), gattn).astype(BF16)
 
+    for start in range(strip, rows - strip, strip):
+        mix(start)
+
+    @pl.when(has_prev)
+    def _():
+        to_next.wait_recv()
+        padded[0:HALO, :] = rms_norm(halo[0].astype(F32), gconv).astype(BF16).astype(F32)
+
+    @pl.when(jnp.logical_not(has_prev))
+    def _():
+        padded[0:HALO, :] = jnp.zeros((HALO, width), F32)
+
+    @pl.when(has_next)
+    def _():
+        to_prev.wait_recv()
+        padded[HALO + rows:, :] = rms_norm(halo[1].astype(F32), gconv).astype(BF16).astype(F32)
+
+    @pl.when(jnp.logical_not(has_next))
+    def _():
+        padded[HALO + rows:, :] = jnp.zeros((HALO, width), F32)
+
+    mix(0)
+    if rows > strip:
+        mix(rows - strip)
+
     loads[0].wait()
     loads[1].wait()
     kv[me, :, 0:key] = dot(attn[...], wk[...]).astype(BF16)
@@ -184,18 +192,21 @@
 
     def attend(pieces, initial):
         keys = jnp.concatenate([kv[s, c * part:(c + 1) * part, 0:key] for s, c in pieces], axis=0)
-        values = jnp.concatenate([kv[s, c * part:(c + 1) * part, key:] for s, c in pieces], axis=0)
-        wide = keys.shape[0] // 128
-
-        @pl.loop(0, HEADS, unroll=2)
+        count = keys.shape[0]
+        wide = count // 128
+        turned[:, 0:count] = keys.T
+        for k, (s, c) in enumerate(pieces):
+            stage[k * part:(k + 1) * part, :] = kv[s, c * part:(c + 1) * part, key:]
+
+        @pl.loop(0, HEADS, unroll=4)
         def _(h):
-            scores = dot_t(q_ref[h], keys)
+            scores = dot(q_ref[h], turned[:, 0:count])
             best = jnp.broadcast_to(jnp.max(scores, axis=1, keepdims=True), (rows, 128))
             if not initial:
                 old = top[h]
                 best = jnp.maximum(old, best)
-            weights = jnp.exp2(scores - jnp.concatenate([best] * wide, axis=1)).astype(BF16)
-            update = dot(weights, values)
+            weights = jnp.exp2((scores - jnp.concatenate([best] * wide, axis=1)).astype(BF16))
+            update = dot(weights, stage[0:count, :])
             if initial:
                 acc[h] = update
             else:
@@ -236,7 +247,7 @@
         both = []
         for h in (pair, pair + 1):
             block = acc[h]
-            both.append((block[:, :val] / block[:, val:val + 1]).astype(BF16))
+            both.append((block[:, :val] * (1.0 / block[:, val:val + 1])).astype(BF16))
         attended[:, pair * val:(pair + 2) * val] = jnp.concatenate(both, axis=1)
 
     loads[3].wait()
@@ -402,6 +413,8 @@
                 pltpu.VMEM((rows, HEADS * val), BF16),
                 pltpu.VMEM((band, channels), BF16),
                 pltpu.VMEM((2, band, channels), BF16),
+                pltpu.VMEM((key, max(4 * rows // PARTS, 2 * rows)), BF16),
+                pltpu.VMEM((max(4 * rows // PARTS, 2 * rows), value_lanes), BF16),
                 dma((len(weights) + 2,)),
                 dma(()),
                 dma((2,)),

time: 57.3 us -> 52.7 us (0.920)
  Pallas kernels: 56.4 us -> 51.6 us
    pallas_call x1, Pallas kernels: 48.4 us -> 43.5 us  [local(): pl.pallas_call(functools.partial(kernel, n), out_shape=(jax.ShapeDtypeStr...]
where the time goes in v3:
time: 52.7 us; the launch traced here: 52.4 us
  Pallas kernels  51.6 us (98%)
  between operations  0.8 us (2%)
    pallas_call x1, Pallas kernels, local(): pl.pallas_call(functools.partial(kernel, n), out_shape=(jax.ShapeDtypeStr...  43.5 us
    pallas_call x1, Pallas kernels, local(): pl.pallas_call(pair_kernel, out_shape=(jax.ShapeDtypeStruct((rows, width)...  8.08 us

profile of v3, /device:TPU:0, one launch (start us, length us, event | category | flops | bytes accessed | tf_op | source)
XLA Modules:
  0.0 52.4 jit_solution(3380992458160098208)
XLA Ops:
  0.6 43.5 %shard_map.122 = (bf16[256,1536]{1,0:T(8,128)(2,1)}, f32[32,128]{1,0:T(8,128)}, bf16[16,16,128]{2,1,0:T(8,128)(2,1)}) custom-call(bf16[256,1536]{1,0:T(8,128)(2,1)} %seq_ref.1, f32[5,1536]{1,0:T(8,128)} %conv_ref.1, f32[1536]{0:T(1024)} %gconv_hbm.1, f32[1536]{0:T(1024)} %gattn_hbm.1, bf16[1536,1024]{1,0:T(8,128)(2,1)} %wq_hbm.1, bf16[1536,128]{1,0:T(8,128)(2,1)} %wk_hbm.1, ...), custom_call_target="tpu_custom_call" | custom-call | tf_op jit(solution)/shard_map/pallas_call | solution.py:392
  44.2 8.1 %shard_map.123 = (bf16[256,1536]{1,0:T(8,128)(2,1)}, bf16[16,256,128]{2,1,0:T(8,128)(2,1)}) custom-call(bf16[256,1536]{1,0:T(8,128)(2,1)} %get-tuple-element.5.track_in, f32[32,128]{1,0:T(8,128)} %get-tuple-element.6.left_ext, bf16[16,16,128]{2,1,0:T(8,128)(2,1)} %get-tuple-element.7.right_land, bf16[1152,128]{1,0:T(8,128)(2,1)} %bitcast.3), custom_call_target="tpu_custom_call" | custom-call | tf_op jit(solution)/shard_map/pallas_call | solution.py:435
